TPU v7x, 128 devices: a whole 4x4x4 slice. The times are simulated.
128 devices in a mesh: seq: 16 (over x_lo, z, core), tp: 8 (over y, x_hi).
Axes of the slice: x: 4 (x_hi: 2, x_lo: 2; x = x_hi * 2 + x_lo), y: 4, z: 4, core: 2. Of those that a mesh axis runs over, the one named last changes fastest.
Arguments:
- hidden_in: bfloat16 [6144, 3584], P('seq'), may hold values from -48 to 48
- joined_inputs: bfloat16 [6144, 8192], P('seq', 'tp'), may hold values from -64 to 64
- lengths: int32 [4], replicated, may hold values from 1 to 3072, 6144 in all
- o_weight: bfloat16 [4096, 3584], P('tp'), may hold values from -0.09375 to 0.09375
- gate_up: float32 [2, 3584, 7168], P(None, ('seq', 'tp')), may hold values from -0.09375 to 0.09375
- down_weight: bfloat16 [7168, 3584], P('tp'), may hold values from -0.0625 to 0.0625
- next_weight: bfloat16 [3584, 8192], P(None, 'tp'), may hold values from -0.09375 to 0.09375
- post_attn_gain: float32 [3584], replicated, may hold values from 0.1 to 1.9
- pre_ffw_gain: float32 [3584], replicated, may hold values from 0.1 to 1.9
- post_ffw_gain: float32 [3584], replicated, may hold values from 0.1 to 1.9
- next_gain: float32 [3584], replicated, may hold values from 0.1 to 1.9
Outputs:
- next_qkv: bfloat16 [6144, 8192], P('seq', 'tp')
Inputs may be any that keep to these rules, and one draw needn't show every extreme that they name: The lengths of 4 prompts laid end to end; they sum to 6144 and the longest is exactly 3072.
All inputs are finite; a program needn't handle non-finite values.
Results may differ from a plain program's by a relative error of at most 0.022.
Values may be sent and summed in bfloat16 or wider, within the bound.
A program may use at most 192 MiB of HBM per device.

v0:
```python
import jax
import jax.numpy as jnp
from jax import lax
from jax.sharding import PartitionSpec as P

HEADS = 16
KV_HEADS = 8
HEAD_DIM = 256


def rms_norm(values, gain):
    meansq = jnp.mean(values * values, axis=-1, keepdims=True)
    return values * lax.rsqrt(meansq + 1e-06) * gain


def local(
    hidden_in,
    joined_inputs,
    lengths,
    o_weight,
    gate_up,
    down_weight,
    next_weight,
    post_attn_gain,
    pre_ffw_gain,
    post_ffw_gain,
    next_gain,
):
    seq_count = lax.axis_size("seq")
    tp_count = lax.axis_size("tp")
    row_count = hidden_in.shape[0]
    model_width = hidden_in.shape[1]
    per_group = HEADS // KV_HEADS
    group_cols = (per_group + 2) * HEAD_DIM
    local_groups = joined_inputs.shape[1] // group_cols
    grouped = joined_inputs.reshape(row_count, local_groups, group_cols)
    queries = grouped[:, :, : per_group * HEAD_DIM].reshape(
        row_count, local_groups, per_group, HEAD_DIM
    )
    own_keys = grouped[:, :, per_group * HEAD_DIM : (per_group + 1) * HEAD_DIM]
    own_values = grouped[:, :, (per_group + 1) * HEAD_DIM :]
    keys_all, values_all = (
        lax.all_gather(own_keys, "seq", axis=0, tiled=True),
        lax.all_gather(own_values, "seq", axis=0, tiled=True),
    )
    total_rows = keys_all.shape[0]
    seq_index = lax.axis_index("seq")
    position = seq_index * row_count
    ends = jnp.cumsum(lengths)
    places = jnp.arange(total_rows, dtype=jnp.int32)
    prompt_ids = jnp.sum((places[:, None] >= ends[None, :]).astype(jnp.int32), axis=1)
    query_place = position + jnp.arange(row_count, dtype=jnp.int32)
    query_ids = lax.dynamic_slice_in_dim(prompt_ids, position, row_count, 0)
    scale = HEAD_DIM ** (-0.5)
    scores = (
        jnp.einsum("qgrd,kgd->qgrk", queries, keys_all, preferred_element_type=jnp.float32) * scale
    )
    allowed = (
        (query_ids[:, None] == prompt_ids[None, :]) & (places[None, :] <= query_place[:, None])
    )[:, None, None, :]
    scores = jnp.where(allowed, scores, -jnp.inf)
    peak = jnp.max(scores, axis=-1, keepdims=True)
    weights = jnp.where(allowed, jnp.exp(scores - peak), 0.0)
    norm_sum = jnp.sum(weights, axis=-1)
    blended = jnp.einsum(
        "qgrk,kgd->qgrd",
        weights.astype(jnp.bfloat16),
        values_all,
        preferred_element_type=jnp.float32,
    )
    blended = blended / norm_sum[..., None]
    attended = blended.astype(jnp.bfloat16).reshape(row_count, local_groups * per_group * HEAD_DIM)
    projected = jnp.dot(attended, o_weight, preferred_element_type=jnp.float32)

    def total_of(values):
        return lax.psum(values.astype(jnp.bfloat16), "tp").astype(jnp.float32)

    residual_mid = hidden_in.astype(jnp.float32) + rms_norm(total_of(projected), post_attn_gain)
    ffw_in = rms_norm(residual_mid, pre_ffw_gain).astype(jnp.bfloat16)
    server_low = gate_up.astype(jnp.bfloat16)
    stacked_rows = lax.all_gather(server_low, "seq", axis=1, tiled=True)
    local_units = lax.all_to_all(stacked_rows, "tp", split_axis=2, concat_axis=1, tiled=True)
    piece_rows = gate_up.shape[1]
    reordered = (
        ffw_in.reshape(row_count, seq_count, tp_count, piece_rows)
        .transpose(0, 2, 1, 3)
        .reshape(row_count, model_width)
    )
    gate = jnp.dot(reordered, local_units[0], preferred_element_type=jnp.float32)
    up_part = jnp.dot(reordered, local_units[1], preferred_element_type=jnp.float32)
    activated = (jax.nn.gelu(gate, approximate=True) * up_part).astype(jnp.bfloat16)
    ffw_out = jnp.dot(activated, down_weight, preferred_element_type=jnp.float32)
    residual_out = residual_mid + rms_norm(total_of(ffw_out), post_ffw_gain)
    next_in = rms_norm(residual_out, next_gain).astype(jnp.bfloat16)
    return jnp.dot(next_in, next_weight, preferred_element_type=jnp.float32).astype(jnp.bfloat16)


def solution(mesh):
    in_specs = (
        P("seq", None),
        P("seq", "tp"),
        P(),
        P("tp", None),
        P(None, ("seq", "tp"), None),
        P("tp", None),
        P(None, "tp"),
        P(),
        P(),
        P(),
        P(),
    )
    out_specs = P("seq", "tp")
    return jax.shard_map(local, mesh=mesh, in_specs=in_specs, out_specs=out_specs, check_vma=False)
```

profile of v0, /device:TPU:1, one launch (start us, length us, event | category | flops | bytes accessed | tf_op | source)
XLA Modules:
  0.0 658.8 jit_solution(18442453555862474000)
XLA Ops:
  6.5 0.0 all-gather.8.cloned.1.call-start
  6.5 2.9 convert_element_type.50
  9.4 0.0 all-gather.8.cloned.1.call-update
  9.4 0.0 all-gather.4.cloned.1.call-start
  9.5 1.8 fusion.53
  11.3 0.0 all-gather.4.cloned.1.call-update
  11.3 0.0 all-gather.6.cloned.1.call-start
  11.4 0.7 all-gather.6.cloned.1.call-update
  12.1 1.0 slice.23
  13.1 0.8 reduce-window.8
  13.9 0.2 copy.49
  14.1 0.1 convert_reduce_fusion
  14.3 0.1 dynamic_slice.3
  14.4 72.0 %all-gather.8.cloned.1.call-done = bf16[2,448,7168]{2,0,1:T(2,128)(2,1)} async-done(((bf16[2,28,7168]{2,0,1:T(2,128)(2,1)}), bf16[2,448,7168]{2,0,1:T(2,128)(2,1)}) %all-gather.8.cloned.1.call-update) | async-done | bytes 12845072 | tf_op jit(solution)/shard_map/all_gather | solution.py:81
  86.4 48.5 %copy.55 = bf16[2,448,7168]{1,0,2:T(2,128)(2,1)} copy(bf16[2,448,7168]{2,0,1:T(2,128)(2,1)} %all-gather.8.cloned.1.call-done) | data formatting | bytes 25690112 | tf_op jit(solution)/shard_map/all_gather | solution.py:81
  134.9 6.5 all-to-all-start
  141.4 0.0 all-reduce.3.cloned.1.call-start
  141.5 3.8 fusion.6
  145.2 0.0 all-gather.4.cloned.1.call-done
  145.2 5.4 fusion
  150.7 0.0 copy-start.2
  150.7 6.5 copy-done.2
  157.2 6.1 fusion.1
  163.3 4.7 all-gather.6.cloned.1.call-done
  167.9 0.0 copy-start.4
  167.9 13.2 %fusion.39 = bf16[1,256,384,2]{2,1,3,0:T(8,128)(2,1)S(1)} fusion(bf16[6144,1,256]{2,0,1:T(8,128)(2,1)} %all-gather.6.cloned.1.call-done, f32[6144,384,2]{1,0,2:T(8,128)} %copy-done.2, f32[384,2]{0,1:T(2,128)S(1)} %get-tuple-element.9, pred[384,6144]{0,1:T(8,128)(4,1)} %fusion.6, f32[384,2]{0,1:T(2,128)S(1)} %fusion.1), kind=kOutput, calls=%fused_computation.45 | convolution fusion | flops 2439905280 | bytes 24778752 | tf_op jit(solution)/shard_map/qgrk,kgd->qgrd/dot_general | solution.py:65
  181.1 0.0 copy-done.4
  181.1 0.0 copy-start.5
  181.2 3.2 convolution_convert_fusion
  184.3 0.0 copy-start.6
  184.3 0.0 all-reduce.3.cloned.1.call-update
  184.4 0.2 all-reduce.5.cloned.1.call-start
  184.6 232.3 %all-reduce.3.cloned.1.call-done = bf16[384,3584]{1,0:T(8,128)(2,1)} async-done(((bf16[384,3584]{1,0:T(8,128)(2,1)}), bf16[384,3584]{1,0:T(8,128)(2,1)}) %all-reduce.3.cloned.1.call-update) | async-done | bytes 2752528 | tf_op jit(solution)/shard_map/psum | solution.py:76
  416.9 0.0 copy-start
  416.9 2.5 fusion.8
  419.5 0.0 copy-done.5
  419.5 4.0 multiply_reduce_fusion.1
  423.5 0.0 copy-done.6
  423.5 0.0 copy-done
  423.5 5.1 multiply_convert_fusion.1
  428.7 4.5 copy.53
  433.2 5.2 reshape.159
  438.4 4.0 copy.54
  442.4 5.2 reshape.160
  447.6 0.0 all-to-all-done
  447.6 24.5 %copy.63 = bf16[2,448,8,896]{3,2,1,0:T(8,128)(2,1)} copy(bf16[2,448,8,896]{1,0,3,2:T(2,128)(2,1)} %bitcast.16) | data formatting | bytes 25690112 | tf_op jit(solution)/shard_map/all_to_all | solution.py:82
  472.1 8.3 %fusion.52 = (bf16[1,8,448,896]{3,1,2,0:T(8,128)(2,1)}, bf16[1,8,448,896]{3,1,2,0:T(8,128)(2,1)S(1)}) fusion(bf16[2,8,448,896]{3,1,2,0:T(8,128)(2,1)} %bitcast.80), kind=kLoop, calls=%fused_computation.60 | loop fusion | bytes 25690112 | tf_op jit(solution)/shard_map/slice | solution.py:89
  480.4 3.9 copy.57
  484.3 3.8 copy.58
  488.1 5.9 fusion.54
  494.0 13.5 %convolution_convert_fusion.1 = bf16[384,3584]{1,0:T(8,128)(2,1)} fusion(bf16[896,3584]{1,0:T(8,128)(2,1)} %param.16, bf16[384,3584]{0,1:T(8,128)(2,1)} %reshape.160, bf16[3584,896]{1,0:T(8,128)(2,1)} %bitcast.83, f32[384,896]{1,0:T(8,128)} %fusion.54), kind=kOutput, calls=%fused_computation.15 | convolution fusion | flops 4937318400 | bytes 19726336 | tf_op jit(solution)/shard_map/dot_general | solution.py:92
  507.4 0.0 copy-start.7
  507.4 0.0 all-reduce.5.cloned.1.call-update
  507.5 0.0 copy-start.8
  507.5 129.4 %all-reduce.5.cloned.1.call-done = bf16[384,3584]{1,0:T(8,128)(2,1)} async-done(((bf16[384,3584]{1,0:T(8,128)(2,1)}), bf16[384,3584]{1,0:T(8,128)(2,1)}) %all-reduce.5.cloned.1.call-update) | async-done | bytes 2752528 | tf_op jit(solution)/shard_map/psum | solution.py:76
  636.9 0.0 copy-start.1
  636.9 0.0 copy-start.3
  636.9 2.5 fusion.11
  639.5 0.0 copy-done.7
  639.5 4.8 multiply_reduce_fusion
  644.3 0.0 copy-done.8
  644.3 0.0 copy-done.1
  644.3 0.0 copy-done.3
  644.3 8.0 %fusion.20 = bf16[384,1024]{1,0:T(8,128)(2,1)} fusion(bf16[3584,1024]{1,0:T(8,128)(2,1)} %param.17, f32[3584]{0:T(1024)S(1)} %copy-done.8, f32[384]{0:T(512)S(1)} %add_rsqrt_fusion, bf16[384,3584]{1,0:T(8,128)(2,1)S(1)} %copy-done.3, bf16[384,3584]{1,0:T(8,128)(2,1)S(1)} %copy-done, bf16[384,3584]{1,0:T(8,128)(2,1)S(1)} %copy-done.1, ...), kind=kOutput, calls=%fused_computation.34 | convolution fusion | flops 2835480576 | bytes 16431616 | tf_op jit(solution)/shard_map/dot_general | solution.py:95
  (5 shorter events, 0.0 us)
Async XLA Ops:
  6.5 79.8 %all-gather.8.cloned.1.call-start = ((), (), s32[]{:S(2)}) async-start(), calls=%async_computation.4 | async-start | bytes 13647872 | tf_op jit(solution)/shard_map/all_gather | solution.py:81
  9.4 135.8 %all-gather.4.cloned.1.call-start = ((), (), s32[]{:S(2)}) async-start(), calls=%async_computation.1 | async-start | bytes 3342336 | tf_op jit(solution)/shard_map/all_gather | solution.py:43
  11.3 156.6 %all-gather.6.cloned.1.call-start = ((), (), s32[]{:S(2)}) async-start(), calls=%async_computation.2 | async-start | bytes 3342336 | tf_op jit(solution)/shard_map/all_gather | solution.py:44
  134.9 312.7 %all-to-all-start = ((bf16[2,448,7168]{1,0,2:T(2,128)(2,1)}), bf16[2,448,7168]{1,0,2:T(2,128)(2,1)}, u32[]{:S(2)}, u32[]{:S(2)}) async-start(bf16[2,448,7168]{1,0,2:T(2,128)(2,1)} %copy.55), calls=%async_computation | async-start | bytes 29360128 | tf_op jit(solution)/shard_map/all_to_all | solution.py:82
  141.4 275.5 %all-reduce.3.cloned.1.call-start = ((), (), s32[]{:S(2)}) async-start(), calls=%async_computation.3 | async-start | bytes 5505024 | tf_op jit(solution)/shard_map/psum | solution.py:76
  150.7 6.5 copy-start.2
  167.9 13.2 %copy-start.4 = (bf16[512,3584]{1,0:T(8,128)(2,1)S(1)}, bf16[512,3584]{1,0:T(8,128)(2,1)}, u32[]{:S(2)}) copy-start(bf16[512,3584]{1,0:T(8,128)(2,1)} %param.14) | copy-start | bytes 11010052
  181.1 238.4 %copy-start.5 = (f32[3584]{0:T(1024)S(1)}, f32[3584]{0:T(1024)}, u32[]{:S(2)}) copy-start(f32[3584]{0:T(1024)} %param.18) | copy-start | bytes 43012
  184.3 239.2 %copy-start.6 = (f32[3584]{0:T(1024)S(1)}, f32[3584]{0:T(1024)}, u32[]{:S(2)}) copy-start(f32[3584]{0:T(1024)} %param.19) | copy-start | bytes 43012
  184.4 452.5 %all-reduce.5.cloned.1.call-start = ((), (), s32[]{:S(2)}) async-start(), calls=%async_computation.5 | async-start | bytes 5505024 | tf_op jit(solution)/shard_map/psum | solution.py:76
  416.9 6.6 copy-start
  507.4 132.0 %copy-start.7 = (f32[3584]{0:T(1024)S(1)}, f32[3584]{0:T(1024)}, u32[]{:S(2)}) copy-start(f32[3584]{0:T(1024)} %param.20) | copy-start | bytes 43012
  507.5 136.8 %copy-start.8 = (f32[3584]{0:T(1024)S(1)}, f32[3584]{0:T(1024)}, u32[]{:S(2)}) copy-start(f32[3584]{0:T(1024)} %param.21) | copy-start | bytes 43012
  636.9 7.4 %copy-start.1 = (bf16[384,3584]{1,0:T(8,128)(2,1)S(1)}, bf16[384,3584]{1,0:T(8,128)(2,1)}, u32[]{:S(2)}) copy-start(bf16[384,3584]{1,0:T(8,128)(2,1)} %param.11) | copy-start | bytes 8257540
  636.9 7.4 %copy-start.3 = (bf16[384,3584]{1,0:T(8,128)(2,1)S(1)}, bf16[384,3584]{1,0:T(8,128)(2,1)}, u32[]{:S(2)}) copy-start(bf16[384,3584]{1,0:T(8,128)(2,1)} %all-reduce.5.cloned.1.call-done) | copy-start | bytes 8257540
Sparse Core Ops, SparseCore 0:
  9.6 76.7 all-gather.7
  88.1 37.0 all-gather.3
  126.8 41.0 all-gather.5
  184.5 232.4 all-reduce.2
  507.6 129.2 all-reduce.4
where the time goes:
time: 662 us; the launch traced here: 659 us
  waiting for transfers between devices  439 us (66%)
  local copies, waits for them, and re-layouts  118 us (18%)
  matrix products  49.1 us (7%)
  other arithmetic  32.8 us (5%)
  between operations  13.3 us (2%)
  starting transfers between devices  6.85 us (1%)
    psum x2, waiting for transfers between devices, total_of(): return lax.psum(values.astype(jnp.bfloat16), 'tp').astype(jnp.float32)  362 us
    all_gather x1, waiting for transfers between devices, local(): stacked_rows = lax.all_gather(server_low, 'seq', axis=1, tiled=True)  72 us
    all_gather x1, local copies, waits for them, and re-layouts, local(): stacked_rows = lax.all_gather(server_low, 'seq', axis=1, tiled=True)  48.5 us
    all_to_all x1, local copies, waits for them, and re-layouts, local(): lax.all_to_all(stacked_rows, 'tp', split_axis=2, concat_axis=1, tiled=True)  24.5 us
    reduce_sum x4, other arithmetic, rms_norm(): meansq = jnp.mean(values * values, axis=-1, keepdims=True)  13.9 us
    dot_general x1, matrix products, local(): jnp.dot(activated, down_weight, preferred_element_type=jnp.float32)  13.5 us
  transfers between devices with their start and end apart: 6, of which 4 were waited for; matrix products, arithmetic and copies ran while one was open for 17% of the time, Pallas kernels for 0%

commit v1 on v0

--- a/solution.py
+++ b/solution.py
@@ -78,7 +78,9 @@
     residual_mid = hidden_in.astype(jnp.float32) + rms_norm(total_of(projected), post_attn_gain)
     ffw_in = rms_norm(residual_mid, pre_ffw_gain).astype(jnp.bfloat16)
     server_low = gate_up.astype(jnp.bfloat16)
-    stacked_rows = lax.all_gather(server_low, "seq", axis=1, tiled=True)
+    stacked_rows = jnp.concatenate(
+        lax.all_to_all(jnp.stack([server_low] * lax.axis_size("seq")), "seq", 0, 0), axis=1
+    )
     local_units = lax.all_to_all(stacked_rows, "tp", split_axis=2, concat_axis=1, tiled=True)
     piece_rows = gate_up.shape[1]
     reordered = (

time: 662 us -> 782 us (1.18)
  waiting for transfers between devices: 439 us -> 547 us
    all_to_all x0 -> x1, waiting for transfers between devices: none -> 188 us  [local(): lax.all_to_all(jnp.stack([server_low] * lax.axis_size('seq')), 'seq', 0, 0)]
    all_gather x1 -> x0, waiting for transfers between devices: 72 us -> none  [local(): stacked_rows = lax.all_gather(server_low, 'seq', axis=1, tiled=True)]
    reshape x0 -> x1, local copies, waits for them, and re-layouts: none -> 48.5 us  [local(): jnp.concatenate(lax.all_to_all(jnp.stack([server_low] * lax.axis_size('se...]
    all_gather x1 -> x0, local copies, waits for them, and re-layouts: 48.5 us -> none  [local(): stacked_rows = lax.all_gather(server_low, 'seq', axis=1, tiled=True)]
    another operation x0 -> x1, local copies, waits for them, and re-layouts: none -> 8.52 us  [local(): jnp.stack([server_low] * lax.axis_size('seq'))]
    all_to_all x0 -> x1, starting transfers between devices: none -> 7.89 us  [local(): lax.all_to_all(jnp.stack([server_low] * lax.axis_size('seq')), 'seq', 0, 0)]
  transfers between devices with their start and end apart: 6 -> 6, of which waited for: 4 -> 3; matrix products, arithmetic and copies ran while one was open for 17% -> 14% of each run, Pallas kernels for 0% -> 0%
where the time goes in v1:
time: 782 us; the launch traced here: 779 us
  waiting for transfers between devices  547 us (70%)
  local copies, waits for them, and re-layouts  124 us (16%)
  matrix products  49.1 us (6%)
  other arithmetic  31.2 us (4%)
  starting transfers between devices  14.4 us (2%)
  between operations  13.3 us (2%)
    psum x2, waiting for transfers between devices, total_of(): return lax.psum(values.astype(jnp.bfloat16), 'tp').astype(jnp.float32)  358 us
    all_to_all x1, waiting for transfers between devices, local(): lax.all_to_all(jnp.stack([server_low] * lax.axis_size('seq')), 'seq', 0, 0)  188 us
    reshape x1, local copies, waits for them, and re-layouts, local(): jnp.concatenate(lax.all_to_all(jnp.stack([server_low] * lax.axis_size('se...  48.5 us
    all_to_all x1, local copies, waits for them, and re-layouts, local(): lax.all_to_all(stacked_rows, 'tp', split_axis=2, concat_axis=1, tiled=True)  24.5 us
  transfers between devices with their start and end apart: 6, of which 3 were waited for; matrix products, arithmetic and copies ran while one was open for 14% of the time, Pallas kernels for 0%

profile of v1, /device:TPU:1, one launch (start us, length us, event | category | flops | bytes accessed | tf_op | source)
XLA Modules:
  0.0 779.3 jit_solution(4079607886459341114)
XLA Ops:
  6.5 2.0 convert_element_type.50
  8.5 8.5 %stack.2 = bf16[16,2,28,7168]{3,1,2,0:T(2,128)(2,1)} broadcast(bf16[2,28,7168]{2,0,1:T(2,128)(2,1)S(1)} %convert_element_type.50), dimensions={1,2,3} | broadcast | bytes 13647872 | tf_op jit(solution)/shard_map/stack | solution.py:82
  17.0 0.0 copy-start.5
  17.0 0.0 copy-start.10
  17.0 7.9 %all-to-all-start = ((bf16[16,2,28,7168]{3,1,2,0:T(2,128)(2,1)}), bf16[16,2,28,7168]{3,1,2,0:T(2,128)(2,1)}, u32[]{:S(2)}, u32[]{:S(2)}) async-start(bf16[16,2,28,7168]{3,1,2,0:T(2,128)(2,1)} %stack.2), calls=%async_computation | async-start | bytes 25690112 | tf_op jit(solution)/shard_map/all_to_all | solution.py:82
  24.9 0.0 all-gather.3.cloned.1.call-start
  25.0 0.0 copy-done.5
  25.0 0.8 fusion.53
  25.8 0.0 all-gather.3.cloned.1.call-update
  25.8 0.0 all-gather.5.cloned.1.call-start
  25.8 0.7 all-gather.5.cloned.1.call-update
  26.6 0.0 copy-done.10
  26.6 0.2 reduce-window.8
  26.8 0.2 copy.49
  27.0 0.1 convert_reduce_fusion
  27.1 0.1 dynamic_slice.3
  27.2 188.3 %all-to-all-done = bf16[16,2,28,7168]{3,1,2,0:T(2,128)(2,1)} async-done(((bf16[16,2,28,7168]{3,1,2,0:T(2,128)(2,1)}), bf16[16,2,28,7168]{3,1,2,0:T(2,128)(2,1)}, u32[]{:S(2)}, u32[]{:S(2)}) %all-to-all-start) | async-done | bytes 12845088 | tf_op jit(solution)/shard_map/all_to_all | solution.py:82
  215.6 48.5 %copy.55 = bf16[2,448,7168]{1,0,2:T(2,128)(2,1)} copy(bf16[2,448,7168]{2,0,1:T(2,128)(2,1)} %bitcast.17) | data formatting | bytes 25690112 | tf_op jit(solution)/shard_map/reshape | solution.py:81
  264.1 6.1 all-to-all-start.1
  270.3 0.0 all-reduce.3.cloned.1.call-start
  270.3 3.8 fusion.6
  274.1 0.0 all-gather.3.cloned.1.call-done
  274.1 5.4 fusion
  279.5 0.0 copy-start.2
  279.5 6.5 copy-done.2
  286.0 6.1 fusion.1
  292.1 0.0 all-gather.5.cloned.1.call-done
  292.1 0.0 copy-start.4
  292.1 13.2 %fusion.39 = bf16[1,256,384,2]{2,1,3,0:T(8,128)(2,1)S(1)} fusion(bf16[6144,1,256]{2,0,1:T(8,128)(2,1)} %all-gather.5.cloned.1.call-done, f32[6144,384,2]{1,0,2:T(8,128)} %copy-done.2, f32[384,2]{0,1:T(2,128)S(1)} %get-tuple-element.9, pred[384,6144]{0,1:T(8,128)(4,1)} %fusion.6, f32[384,2]{0,1:T(2,128)S(1)} %fusion.1), kind=kOutput, calls=%fused_computation.45 | convolution fusion | flops 2439905280 | bytes 24778752 | tf_op jit(solution)/shard_map/qgrk,kgd->qgrd/dot_general | solution.py:65
  305.3 0.0 copy-done.4
  305.3 0.0 copy-start.6
  305.3 3.2 convolution_convert_fusion
  308.5 0.0 copy-start.7
  308.5 0.0 all-reduce.3.cloned.1.call-update
  308.6 0.2 all-reduce.5.cloned.1.call-start
  308.8 228.1 %all-reduce.3.cloned.1.call-done = bf16[384,3584]{1,0:T(8,128)(2,1)} async-done(((bf16[384,3584]{1,0:T(8,128)(2,1)}), bf16[384,3584]{1,0:T(8,128)(2,1)}) %all-reduce.3.cloned.1.call-update) | async-done | bytes 2752528 | tf_op jit(solution)/shard_map/psum | solution.py:76
  536.9 0.0 copy-start
  536.9 2.5 fusion.8
  539.4 0.0 copy-done.6
  539.4 4.0 multiply_reduce_fusion.1
  543.4 0.0 copy-done.7
  543.5 0.0 copy-done
  543.5 5.1 multiply_convert_fusion.1
  548.6 4.5 copy.53
  553.1 5.2 reshape.167
  558.3 4.0 copy.54
  562.4 5.2 reshape.168
  567.6 0.0 all-to-all-done.1
  567.6 24.5 %copy.63 = bf16[2,448,8,896]{3,2,1,0:T(8,128)(2,1)} copy(bf16[2,448,8,896]{1,0,3,2:T(2,128)(2,1)} %bitcast.18) | data formatting | bytes 25690112 | tf_op jit(solution)/shard_map/all_to_all | solution.py:84
  592.1 8.3 %fusion.52 = (bf16[1,8,448,896]{3,1,2,0:T(8,128)(2,1)}, bf16[1,8,448,896]{3,1,2,0:T(8,128)(2,1)S(1)}) fusion(bf16[2,8,448,896]{3,1,2,0:T(8,128)(2,1)} %bitcast.83), kind=kLoop, calls=%fused_computation.60 | loop fusion | bytes 25690112 | tf_op jit(solution)/shard_map/slice | solution.py:91
  600.3 3.9 copy.57
  604.2 3.8 copy.58
  608.0 5.9 fusion.54
  613.9 13.4 %convolution_convert_fusion.1 = bf16[384,3584]{1,0:T(8,128)(2,1)} fusion(bf16[896,3584]{1,0:T(8,128)(2,1)} %param.16, bf16[384,3584]{0,1:T(8,128)(2,1)} %reshape.168, bf16[3584,896]{1,0:T(8,128)(2,1)} %bitcast.86, f32[384,896]{1,0:T(8,128)} %fusion.54), kind=kOutput, calls=%fused_computation.15 | convolution fusion | flops 4937318400 | bytes 19726336 | tf_op jit(solution)/shard_map/dot_general | solution.py:94
  627.4 0.0 all-reduce.5.cloned.1.call-update
  627.4 0.0 copy-start.9
  627.4 130.0 %all-reduce.5.cloned.1.call-done = bf16[384,3584]{1,0:T(8,128)(2,1)} async-done(((bf16[384,3584]{1,0:T(8,128)(2,1)}), bf16[384,3584]{1,0:T(8,128)(2,1)}) %all-reduce.5.cloned.1.call-update) | async-done | bytes 2752528 | tf_op jit(solution)/shard_map/psum | solution.py:76
  757.4 2.5 fusion.11
  759.9 0.0 copy-done.8
  759.9 4.8 multiply_reduce_fusion
  764.7 0.0 copy-done.9
  764.8 0.0 copy-done.1
  764.8 0.0 copy-done.3
  764.8 8.0 %fusion.20 = bf16[384,1024]{1,0:T(8,128)(2,1)} fusion(bf16[3584,1024]{1,0:T(8,128)(2,1)} %param.17, f32[3584]{0:T(1024)S(1)} %copy-done.9, f32[384]{0:T(512)S(1)} %add_rsqrt_fusion, bf16[384,3584]{1,0:T(8,128)(2,1)S(1)} %copy-done.3, bf16[384,3584]{1,0:T(8,128)(2,1)S(1)} %copy-done, bf16[384,3584]{1,0:T(8,128)(2,1)S(1)} %copy-done.1, ...), kind=kOutput, calls=%fused_computation.34 | convolution fusion | flops 2835480576 | bytes 16431616 | tf_op jit(solution)/shard_map/dot_general | solution.py:97
  (9 shorter events, 0.1 us)
Async XLA Ops:
  17.0 7.9 %copy-start.5 = (bf16[384,1024]{1,0:T(8,128)(2,1)S(1)}, bf16[384,1024]{1,0:T(8,128)(2,1)}, u32[]{:S(2)}) copy-start(bf16[384,1024]{1,0:T(8,128)(2,1)} %param.12) | copy-start | bytes 2359300
  17.0 9.6 %copy-start.10 = (s32[4]{0:T(128)S(1)}, s32[4]{0:T(128)}, u32[]{:S(2)}) copy-start(s32[4]{0:T(128)} %param.13) | copy-start | bytes 52
  17.0 198.5 %all-to-all-start = ((bf16[16,2,28,7168]{3,1,2,0:T(2,128)(2,1)}), bf16[16,2,28,7168]{3,1,2,0:T(2,128)(2,1)}, u32[]{:S(2)}, u32[]{:S(2)}) async-start(bf16[16,2,28,7168]{3,1,2,0:T(2,128)(2,1)} %stack.2), calls=%async_computation | async-start | bytes 25690112 | tf_op jit(solution)/shard_map/all_to_all | solution.py:82
  24.9 249.2 %all-gather.3.cloned.1.call-start = ((), (), s32[]{:S(2)}) async-start(), calls=%async_computation.2 | async-start | bytes 3342336 | tf_op jit(solution)/shard_map/all_gather | solution.py:43
  25.8 266.3 %all-gather.5.cloned.1.call-start = ((), (), s32[]{:S(2)}) async-start(), calls=%async_computation.3 | async-start | bytes 3342336 | tf_op jit(solution)/shard_map/all_gather | solution.py:44
  264.1 303.5 %all-to-all-start.1 = ((bf16[2,448,7168]{1,0,2:T(2,128)(2,1)}), bf16[2,448,7168]{1,0,2:T(2,128)(2,1)}, u32[]{:S(2)}, u32[]{:S(2)}) async-start(bf16[2,448,7168]{1,0,2:T(2,128)(2,1)} %copy.55), calls=%async_computation.1 | async-start | bytes 29360128 | tf_op jit(solution)/shard_map/all_to_all | solution.py:84
  270.3 266.6 %all-reduce.3.cloned.1.call-start = ((), (), s32[]{:S(2)}) async-start(), calls=%async_computation.4 | async-start | bytes 5505024 | tf_op jit(solution)/shard_map/psum | solution.py:76
  279.5 6.5 copy-start.2
  292.1 13.2 %copy-start.4 = (bf16[512,3584]{1,0:T(8,128)(2,1)S(1)}, bf16[512,3584]{1,0:T(8,128)(2,1)}, u32[]{:S(2)}) copy-start(bf16[512,3584]{1,0:T(8,128)(2,1)} %param.14) | copy-start | bytes 11010052
  305.3 234.1 %copy-start.6 = (f32[3584]{0:T(1024)S(1)}, f32[3584]{0:T(1024)}, u32[]{:S(2)}) copy-start(f32[3584]{0:T(1024)} %param.18) | copy-start | bytes 43012
  308.5 234.9 %copy-start.7 = (f32[3584]{0:T(1024)S(1)}, f32[3584]{0:T(1024)}, u32[]{:S(2)}) copy-start(f32[3584]{0:T(1024)} %param.19) | copy-start | bytes 43012
  308.6 448.8 %all-reduce.5.cloned.1.call-start = ((), (), s32[]{:S(2)}) async-start(), calls=%async_computation.5 | async-start | bytes 5505024 | tf_op jit(solution)/shard_map/psum | solution.py:76
  536.9 6.6 copy-start
  627.3 132.6 %copy-start.8 = (f32[3584]{0:T(1024)S(1)}, f32[3584]{0:T(1024)}, u32[]{:S(2)}) copy-start(f32[3584]{0:T(1024)} %param.20) | copy-start | bytes 43012
  627.4 137.4 %copy-start.9 = (f32[3584]{0:T(1024)S(1)}, f32[3584]{0:T(1024)}, u32[]{:S(2)}) copy-start(f32[3584]{0:T(1024)} %param.21) | copy-start | bytes 43012
  757.4 7.4 copy-start.1
  757.4 7.4 copy-start.3
Sparse Core Ops, SparseCore 0:
  27.5 146.7 all-gather.2
  175.9 60.0 all-gather.4
  308.7 228.1 all-reduce.2
  627.5 129.8 all-reduce.4
